TPU v7x, 32 devices: a whole 2x2x4 slice. The times are simulated.
32 devices in a mesh: groups: 2 (over x), blk: 16 (over z, y, core).
Axes of the slice: x: 2, y: 2, z: 4, core: 2. Of those that a mesh axis runs over, the one named last changes fastest.
Arguments:
- text_queries: bfloat16 [4096, 4096], P(('groups', 'blk')), parts along dimension 0, may hold values from -170 to 170
- image_states: bfloat16 [1536, 8192], P(('groups', 'blk')), parts along dimension 0, may hold values from -6 to 6
- kv_weight: bfloat16 [8192, 1024], P('blk'), may hold values from -0.1875 to 0.1875
- q_gain: float32 [128], replicated, may hold values from 0.25 to 1.75
- k_gain: float32 [128], replicated, may hold values from 0.25 to 1.75
- text_counts: int32 [6], P('groups'), parts along dimension 0, may hold values from 1 to 1024, 2048 in all
- image_counts: int32 [6], P('groups'), parts along dimension 0, may hold values from 96 to 384, as said below
Outputs:
- attended: bfloat16 [4096, 4096], P(('groups', 'blk')), parts along dimension 0
There are 2 independent parts, one for each index of `groups`. A program takes and returns all parts, laid end to end along the dimension named above; an argument that names none is the same for every part. Nothing has to cross between parts.
Inputs may be any that keep to these rules, and one draw needn't show every extreme that they name: `text_counts`: they sum to 2048. `image_counts`: they sum to 768; the second image has exactly 384 tokens, the first and last are cut by the window.
All inputs are finite; a program needn't handle non-finite values.
Results may differ from a plain program's by a relative error of at most 0.0071.
Values may be sent and summed in bfloat16 or wider, within the bound.
No kernel may reach another device: no remote copies, remote signals or barrier semaphores. Data moves between devices by JAX's collectives and lax.ppermute only.
A program may use at most 128 MiB of HBM per device.

v0:
```python
import math

import jax
import jax.numpy as jnp
from jax import lax
from jax.sharding import PartitionSpec as P

epsilon = 1e-05


def rms_norm(inputs, norm_gain):
    return (
        inputs * lax.rsqrt(jnp.mean(inputs * inputs, axis=-1, keepdims=True) + epsilon) * norm_gain
    )


def body(text_queries, image_states, kv_weight, q_gain, k_gain, text_counts, image_counts):
    head_dim = q_gain.shape[0]
    text_rows = text_queries.shape[0]
    image_rows = image_states.shape[0]
    kv_width = kv_weight.shape[1] // 2
    kv_heads = kv_width // head_dim
    query_heads = text_queries.shape[1] // head_dim
    group_size = query_heads // kv_heads
    columns = lax.all_to_all(image_states, "blk", split_axis=1, concat_axis=0, tiled=True)
    projected = lax.psum_scatter(
        jnp.dot(columns, kv_weight, preferred_element_type=jnp.float32),
        "blk",
        scatter_dimension=0,
        tiled=True,
    )
    image_keys = rms_norm(projected[:, :kv_width].reshape(image_rows, kv_heads, head_dim), k_gain)
    image_keys = image_keys.astype(jnp.bfloat16).reshape(image_rows, kv_width)
    image_values = projected[:, kv_width:].astype(jnp.bfloat16)
    kv_rows_local = jnp.concatenate([image_keys, image_values], axis=1)
    normed_queries = rms_norm(
        text_queries.astype(jnp.float32).reshape(text_rows, query_heads, head_dim), q_gain
    )
    normed_queries = normed_queries.astype(jnp.bfloat16).reshape(
        text_rows, kv_heads, group_size, head_dim
    )
    text_positions = lax.axis_index("blk") * text_rows + jnp.arange(text_rows, dtype=jnp.int32)
    text_ends = jnp.cumsum(text_counts)
    image_ends = jnp.cumsum(image_counts)
    text_segment = jnp.sum(
        (text_ends[None, :] <= text_positions[:, None]).astype(jnp.int32), axis=1
    )
    score_scale = 1.0 / math.sqrt(head_dim)
    arrived = lax.all_gather(kv_rows_local, "blk", axis=0, tiled=True)
    first_row = jnp.int32(0)
    numerator = jnp.zeros((kv_heads, group_size, text_rows, head_dim), jnp.float32)
    denominator = jnp.zeros((kv_heads, group_size, text_rows), jnp.float32)
    key_span = arrived.shape[0]
    for offset in range(0, key_span, 512):
        block_size = min(512, key_span - offset)
        key_block = arrived[offset : offset + block_size]
        key_heads = key_block[:, :kv_width].reshape(block_size, kv_heads, head_dim)
        value_heads = key_block[:, kv_width:].reshape(block_size, kv_heads, head_dim)
        key_positions = first_row + offset + jnp.arange(block_size, dtype=jnp.int32)
        key_owner = jnp.sum(
            (image_ends[None, :] <= key_positions[:, None]).astype(jnp.int32), axis=1
        )
        allowed = key_owner[None, :] <= text_segment[:, None]
        scores = (
            jnp.einsum(
                "tgrd,pgd->grtp", normed_queries, key_heads, preferred_element_type=jnp.float32
            )
            * score_scale
        )
        weights = jnp.where(allowed, jnp.exp(scores), 0.0)
        denominator = denominator + jnp.sum(weights, axis=-1)
        numerator = numerator + jnp.einsum(
            "grtp,pgd->grtd",
            weights.astype(jnp.bfloat16),
            value_heads,
            preferred_element_type=jnp.float32,
        )
    numerator, denominator = (numerator, denominator)
    attended = (numerator / denominator[..., None]).astype(jnp.bfloat16)
    return jnp.transpose(attended, (2, 0, 1, 3)).reshape(text_rows, query_heads * head_dim)


def solution(mesh):
    placed = (
        P(("groups", "blk"), None),
        P(("groups", "blk"), None),
        P("blk", None),
        P(),
        P(),
        P("groups"),
        P("groups"),
    )
    return jax.shard_map(
        body, mesh=mesh, in_specs=placed, out_specs=P(("groups", "blk"), None), check_vma=False
    )
```

profile of v0, /device:TPU:0, one launch (start us, length us, event | category | flops | bytes accessed | tf_op | source)
XLA Modules:
  0.0 173.4 jit_solution(13814516155407754564)
XLA Ops:
  6.5 0.0 copy-start
  6.5 0.0 reduce-scatter.2.cloned.1.call-start
  6.5 1.3 copy.124
  7.8 27.3 %all_to_all.19 = bf16[48,16,512]{2,0,1:T(8,128)(2,1)S(1)} all-to-all(bf16[48,16,512]{2,0,1:T(8,128)(2,1)S(1)} %bitcast.70), channel_id=1, replica_groups=mesh['groups'=2,'blk'=16] {'blk'}, dimensions={1} | all-to-all | bytes 1572864 | tf_op jit(solution)/shard_map/all_to_all | solution.py:25
  35.2 0.0 copy-done
  35.2 2.6 %fusion.34 = f32[768,1024]{1,0:T(8,128)} fusion(bf16[768,512]{1,0:T(8,128)(2,1)S(1)} %bitcast.69, bf16[512,1024]{1,0:T(8,128)(2,1)S(1)} %copy-done), kind=kOutput, calls=%fused_computation.51 | convolution fusion | flops 805306368 | bytes 4980736 | tf_op jit(solution)/shard_map/dot_general | solution.py:27
  37.8 0.0 reduce-scatter.2.cloned.1.call-update
  37.9 0.0 all-gather.2.cloned.1.call-start
  37.9 0.6 copy-done.4
  38.5 65.1 %reduce-scatter.2.cloned.1.call-done = f32[48,1024]{1,0:T(8,128)} async-done(((f32[768,1024]{1,0:T(8,128)}), f32[48,1024]{1,0:T(8,128)}) %reduce-scatter.2.cloned.1.call-update) | async-done | bytes 196624 | tf_op jit(solution)/shard_map/reduce_scatter | solution.py:26
  103.6 0.9 slice_multiply_fusion
  104.5 0.1 reduce_sum.65
  104.7 0.9 slice.40
  105.6 0.1 mul.74
  105.7 0.9 fusion.27
  106.6 0.6 pad_maximum_fusion
  107.3 0.0 all-gather.2.cloned.1.call-update
  107.3 0.0 copy-done.5
  107.3 0.2 reduce-window.17
  107.5 0.0 copy-done.6
  107.5 0.2 reduce-window.16
  107.7 0.0 copy-done.1
  107.7 0.2 fusion.9
  107.9 0.4 copy.101
  108.3 0.6 reduce_sum.66
  108.9 0.1 copy.77
  108.9 1.4 convert_bitcast_fusion
  110.4 0.4 copy.100
  110.8 0.1 convert_reduce_fusion
  110.9 0.1 convert_reduce_fusion.2
  110.9 0.1 convert_reduce_fusion.1
  111.0 0.1 broadcast_compare_fusion.1
  111.2 0.1 broadcast_compare_fusion
  111.3 34.7 %all-gather.2.cloned.1.call-done = bf16[768,1024]{1,0:T(8,128)(2,1)} async-done(((bf16[48,1024]{1,0:T(8,128)(2,1)}), bf16[768,1024]{1,0:T(8,128)(2,1)}) %all-gather.2.cloned.1.call-update) | async-done | bytes 1572880 | tf_op jit(solution)/shard_map/all_gather | solution.py:49
  146.0 2.2 %fusion.32 = (bf16[512,512]{1,0:T(8,128)(2,1)}, bf16[512,512]{1,0:T(8,128)(2,1)}) fusion(bf16[768,1024]{1,0:T(8,128)(2,1)} %all-gather.2.cloned.1.call-done), kind=kLoop, calls=%fused_computation.49 | loop fusion | bytes 2097152 | tf_op jit(solution)/shard_map/slice | solution.py:57
  148.3 2.0 %reshape.123 = bf16[512,4,128]{2,1,0:T(4,128)(2,1)} reshape(bf16[512,512]{1,0:T(8,128)(2,1)} %get-tuple-element.5) | data formatting | bytes 1048576 | tf_op jit(solution)/shard_map/reshape | solution.py:57
  150.2 1.8 %fusion.33 = (bf16[256,512]{1,0:T(8,128)(2,1)S(1)}, bf16[256,512]{1,0:T(8,128)(2,1)}) fusion(bf16[768,1024]{1,0:T(8,128)(2,1)} %all-gather.2.cloned.1.call-done), kind=kLoop, calls=%fused_computation.50 | loop fusion | bytes 1048576 | tf_op jit(solution)/shard_map/slice | solution.py:57
  152.0 0.8 reshape.126
  152.8 1.1 copy.97
  153.9 2.0 %copy.94 = bf16[512,512]{0,1:T(8,128)(2,1)} copy(bf16[512,512]{1,0:T(8,128)(2,1)} %get-tuple-element.6) | data formatting | bytes 1048576 | tf_op jit(solution)/shard_map/reshape | solution.py:58
  155.9 0.0 copy-done.7
  155.9 3.2 %fusion.7 = (f32[4,8,128]{2,1,0:T(8,128)S(1)}, f32[4,256,128,8]{2,1,3,0:T(8,128)S(1)}) fusion(pred[128,256]{0,1:T(8,128)(4,1)S(1)} %broadcast_compare_fusion.1, f32[128,4,8,128]{3,2,1,0:T(8,128)S(1)} %bitcast.71, f32[128]{0:T(128)S(1)} %copy-done.7, f32[128,4,8]{0,2,1:T(8,128)S(1)} %rsqrt_bitcast_fusion, bf16[256,4,128,1]{2,1,0,3:T(4,128)(2,1)} %bitcast.79), kind=kOutput, calls=%fused_computation.8 | convolution fusion | flops 273149952 | bytes 6619648 | tf_op jit(solution)/shard_map/tgrd,pgd->grtp/dot_general | solution.py:65
  159.1 0.0 copy-start.2
  159.1 0.9 fusion.10
  160.0 0.2 copy-done.2
  160.2 3.3 %fusion = (f32[4,8,128]{2,1,0:T(8,128)S(1)}, f32[4,512,128,8]{2,1,3,0:T(8,128)S(1)}) fusion(pred[128,512]{0,1:T(8,128)(4,1)S(1)} %broadcast_compare_fusion, f32[128,4,8,128]{3,2,1,0:T(8,128)S(1)} %bitcast.72, f32[128]{0:T(128)S(1)} %copy-done.7, f32[128,4,8]{0,2,1:T(8,128)S(1)} %rsqrt_bitcast_fusion, bf16[512,4,128,1]{2,1,0,3:T(4,128)(2,1)S(1)} %bitcast.76), kind=kOutput, calls=%fused_computation.1 | convolution fusion | flops 544731136 | bytes 11108864 | tf_op jit(solution)/shard_map/tgrd,pgd->grtp/dot_general | solution.py:65
  163.5 1.8 %fusion.12 = bf16[128,4,8,128]{0,3,2,1:T(8,128)(2,1)S(1)} fusion(f32[4,8,128,128]{2,3,1,0:T(8,128)S(1)} %fusion.10, bf16[512,4,128,1]{0,2,3,1:T(8,128)(2,1)S(1)} %bitcast.77, f32[4,512,128,8]{2,1,3,0:T(8,128)S(1)} %get-tuple-element.10, pred[128,512]{0,1:T(8,128)(4,1)S(1)} %broadcast_compare_fusion, f32[128,4,8]{0,2,1:T(8,128)S(1)} %add_bitcast_fusion), kind=kOutput, calls=%fused_computation.15 | convolution fusion | flops 544735232 | bytes 12140544 | tf_op jit(solution)/shard_map/grtp,pgd->grtd/dot_general | solution.py:72
  165.3 1.3 copy.85
  (14 shorter events, 0.1 us)
Async XLA Ops:
  6.5 28.6 %copy-start = (bf16[512,1024]{1,0:T(8,128)(2,1)S(1)}, bf16[512,1024]{1,0:T(8,128)(2,1)}, u32[]{:S(2)}) copy-start(bf16[512,1024]{1,0:T(8,128)(2,1)} %param.9) | copy-start | bytes 3145732
  6.5 97.0 %reduce-scatter.2.cloned.1.call-start = ((), (), s32[]{:S(2)}) async-start(), calls=%async_computation.2 | async-start | bytes 3342336 | tf_op jit(solution)/shard_map/reduce_scatter | solution.py:26
  37.8 0.7 copy-start.4
  37.8 69.5 %copy-start.5 = (s32[3]{0:T(128)S(1)}, s32[3]{0:T(128)}, u32[]{:S(2)}) copy-start(s32[3]{0:T(128)} %param.12) | copy-start | bytes 40
  37.8 69.6 %copy-start.6 = (s32[3]{0:T(128)S(1)}, s32[3]{0:T(128)}, u32[]{:S(2)}) copy-start(s32[3]{0:T(128)} %param.13) | copy-start | bytes 40
  37.8 69.8 %copy-start.1 = (bf16[128,4096]{1,0:T(8,128)(2,1)S(1)}, bf16[128,4096]{1,0:T(8,128)(2,1)}, u32[]{:S(2)}) copy-start(bf16[128,4096]{1,0:T(8,128)(2,1)} %param.7) | copy-start | bytes 3145732
  37.9 108.2 %all-gather.2.cloned.1.call-start = ((), (), s32[]{:S(2)}) async-start(), calls=%async_computation.3 | async-start | bytes 1671168 | tf_op jit(solution)/shard_map/all_gather | solution.py:49
  148.3 7.7 %copy-start.7 = (f32[128]{0:T(128)S(1)}, f32[128]{0:T(128)}, u32[]{:S(2)}) copy-start(f32[128]{0:T(128)} %param.10) | copy-start | bytes 1540
  159.1 1.0 copy-start.2
  160.2 3.3 %copy-start.3 = (bf16[512,512]{0,1:T(8,128)(2,1)S(1)}, bf16[512,512]{0,1:T(8,128)(2,1)}, u32[]{:S(2)}) copy-start(bf16[512,512]{0,1:T(8,128)(2,1)} %copy.94) | copy-start | bytes 1572868
Sparse Core Ops, SparseCore 0:
  38.0 65.5 reduce-scatter.1
  107.4 38.5 all-gather.1
where the time goes:
time: 174 us; the launch traced here: 173 us
  waiting for transfers between devices  99.9 us (57%)
  blocking collectives  27.3 us (16%)
  local copies, waits for them, and re-layouts  15.1 us (9%)
  between operations  13.6 us (8%)
  matrix products  11.8 us (7%)
  other arithmetic  5.74 us (3%)
    reduce_scatter x1, waiting for transfers between devices, body(): lax.psum_scatter(jnp.dot(columns, kv_weight, preferred_element_type=jnp.f...  65.1 us
    all_gather x1, waiting for transfers between devices, body(): arrived = lax.all_gather(kv_rows_local, 'blk', axis=0, tiled=True)  34.7 us
    all_to_all x1, blocking collectives, body(): lax.all_to_all(image_states, 'blk', split_axis=1, concat_axis=0, tiled=True)  27.3 us
    dot_general x2, matrix products, body(): jnp.einsum('tgrd,pgd->grtp', normed_queries, key_heads, preferred_element...  6.52 us
    slice x2, local copies, waits for them, and re-layouts, body(): key_heads = key_block[:, :kv_width].reshape(block_size, kv_heads, head_dim)  4 us
  transfers between devices with their start and end apart: 2, of which 2 were waited for; matrix products, arithmetic and copies ran while one was open for 2% of the time, Pallas kernels for 0%

commit v1 on v0

v1 whole, which is shorter than its diff:
```python
import functools
import math

import jax
import jax.numpy as jnp
from jax import lax
from jax.experimental import pallas as pl
from jax.experimental.pallas import tpu as pltpu
from jax.sharding import PartitionSpec as P

epsilon = 1e-05
LANE = 4


def norm_kernel(heads, head_dim, x_ref, gain_ref, out_ref):
    gain = gain_ref[...]
    for h in range(heads):
        columns = slice(h * head_dim, (h + 1) * head_dim)
        x = x_ref[:, columns].astype(jnp.float32)
        scale = lax.rsqrt(jnp.mean(x * x, axis=-1, keepdims=True) + epsilon)
        out_ref[:, columns] = (x * scale * gain).astype(out_ref.dtype)


def norm_queries(queries, gain):
    rows, width = queries.shape
    head_dim = gain.shape[-1]
    return pl.pallas_call(
        functools.partial(norm_kernel, width // head_dim, head_dim),
        out_shape=jax.ShapeDtypeStruct((rows, width), jnp.bfloat16),
        name="norm_queries",
    )(queries, gain)


def attend_kernel(group_size, head_dim, n_sets, q_ref, segment_ref, bias_ref, *refs):
    kv_refs, out_ref = refs[:-1], refs[-1]
    k_refs, v_refs = kv_refs[:n_sets], kv_refs[n_sets:]
    rows = q_ref.shape[0]
    segment = segment_ref[...]
    keys = jnp.concatenate([r[...] for r in k_refs], axis=0)
    values = jnp.concatenate([r[...] for r in v_refs], axis=0)
    keys = jnp.concatenate([keys, bias_ref[...]], axis=1)
    values = jnp.concatenate([values, jnp.ones_like(values)], axis=1)
    stack = math.gcd(group_size, 4)
    for first in range(0, group_size, stack):
        spans = [slice(h * head_dim, (h + 1) * head_dim) for h in range(first, first + stack)]
        q = jnp.concatenate(
            [jnp.concatenate([q_ref[:, span], segment], axis=1) for span in spans], axis=0
        )
        scores = lax.dot_general(
            q, keys, (((1,), (1,)), ((), ())), preferred_element_type=jnp.float32
        )
        weights = jnp.exp2(scores).astype(jnp.bfloat16)
        sums = jnp.dot(weights, values, preferred_element_type=jnp.float32)
        result = (sums[:, :head_dim] / sums[:, head_dim:]).astype(out_ref.dtype)
        for i, span in enumerate(spans):
            out_ref[:, span] = result[i * rows : (i + 1) * rows]


def attend(queries, segment, bias, sets, head_dim):
    rows, width = queries.shape
    kv_heads = sets[0].shape[1] // (2 * head_dim)
    group_size = width // head_dim // kv_heads
    span = sets[0].shape[0]
    whole = lambda g: (0, 0)
    return pl.pallas_call(
        functools.partial(attend_kernel, group_size, head_dim, len(sets)),
        grid=(kv_heads,),
        in_specs=[
            pl.BlockSpec((rows, group_size * head_dim), lambda g: (0, g)),
            pl.BlockSpec(segment.shape, whole),
            pl.BlockSpec(bias.shape, whole),
            *[pl.BlockSpec((span, head_dim), lambda g: (0, g)) for _ in sets],
            *[pl.BlockSpec((span, head_dim), lambda g: (0, g + kv_heads)) for _ in sets],
        ],
        out_specs=pl.BlockSpec((rows, group_size * head_dim), lambda g: (0, g)),
        out_shape=jax.ShapeDtypeStruct((rows, width), jnp.bfloat16),
        name="attend",
    )(queries, segment, bias, *sets, *sets)


def body(n_blk, text_queries, image_states, kv_weight, q_gain, k_gain, text_counts, image_counts):
    head_dim = q_gain.shape[0]
    text_rows = text_queries.shape[0]
    image_rows = image_states.shape[0]
    kv_width = kv_weight.shape[1] // 2
    kv_heads = kv_width // head_dim
    depth = kv_weight.shape[0]
    images = text_counts.shape[0]
    planes = n_blk // LANE
    me = lax.axis_index("blk")
    plane, lane = me // LANE, me % LANE

    def swap_lane(x, bits):
        return lax.ppermute(x, "blk", [(i, i ^ bits) for i in range(n_blk)])

    def swap_plane(x, step):
        return lax.ppermute(x, "blk", [(i, i ^ (step * LANE)) for i in range(n_blk)])

    span = LANE * depth
    received = [lax.dynamic_slice_in_dim(image_states, plane * span, span, 1)]
    for step in range(1, planes):
        outgoing = lax.dynamic_slice_in_dim(image_states, (plane ^ step) * span, span, 1)
        received.append(swap_plane(outgoing, step))
    weights = [kv_weight, swap_lane(kv_weight, 1), swap_lane(kv_weight, 2)]
    weights.append(swap_lane(weights[2], 1))

    queries = norm_queries(text_queries, q_gain[None, :])
    positions = me * text_rows + jnp.arange(text_rows, dtype=jnp.int32)
    text_ends, image_ends = jnp.cumsum(text_counts), jnp.cumsum(image_counts)
    text_segment = jnp.sum((text_ends[None, :] <= positions[:, None]).astype(jnp.int32), axis=1)
    slots = -(-(images + 1) // 128) * 128
    slot = jnp.arange(slots, dtype=jnp.int32)
    segment = (text_segment[:, None] == slot[None, :]).astype(jnp.bfloat16)
    r = jnp.arange(image_rows, dtype=jnp.int32)[None, None, :]
    s = jnp.arange(planes, dtype=jnp.int32)[None, :, None]
    j = jnp.arange(LANE, dtype=jnp.int32)[:, None, None]
    image_positions = ((((plane ^ s) * LANE) + (lane ^ j)) * image_rows + r).reshape(-1)
    owner = jnp.sum((image_ends[None, :] <= image_positions[:, None]).astype(jnp.int32), axis=1)
    bias = jnp.where(owner[:, None] <= slot[None, :], 0.0, -30000.0).astype(jnp.bfloat16)
    received, queries, segment, bias = lax.optimization_barrier(
        (received, queries, segment, bias)
    )

    stacked = jnp.concatenate(received, axis=0)
    partial = jnp.zeros((planes * image_rows, 2 * kv_width), jnp.float32)
    for j in range(LANE):
        columns = lax.dynamic_slice_in_dim(stacked, (lane ^ j) * depth, depth, 1)
        partial = partial + jnp.dot(columns, weights[j], preferred_element_type=jnp.float32)
    projected = partial[:image_rows]
    for step in range(1, planes):
        outgoing = partial[step * image_rows : (step + 1) * image_rows].astype(jnp.bfloat16)
        projected = projected + swap_plane(outgoing, step).astype(jnp.float32)
    keys = projected[:, :kv_width].reshape(image_rows, kv_heads, head_dim)
    keys = keys * lax.rsqrt(jnp.mean(keys * keys, axis=-1, keepdims=True) + epsilon)
    keys = keys * (k_gain * (math.log2(math.e) / math.sqrt(head_dim)))
    own = jnp.concatenate([keys.reshape(image_rows, kv_width), projected[:, kv_width:]], axis=1)
    own = own.astype(jnp.bfloat16)

    sets = [jnp.concatenate([own] + [swap_plane(own, s) for s in range(1, planes)], axis=0)]
    sets.append(swap_lane(sets[0], 1))
    sets.append(swap_lane(sets[0], 2))
    sets.append(swap_lane(sets[2], 1))

    return attend(queries, segment, bias, sets, head_dim)


def solution(mesh):
    placed = (
        P(("groups", "blk"), None),
        P(("groups", "blk"), None),
        P("blk", None),
        P(),
        P(),
        P("groups"),
        P("groups"),
    )
    return jax.shard_map(
        functools.partial(body, mesh.shape["blk"]),
        mesh=mesh,
        in_specs=placed,
        out_specs=P(("groups", "blk"), None),
        check_vma=False,
    )
```

time: 174 us -> 75.4 us (0.43)
  waiting for transfers between devices: 99.9 us -> 36.8 us
  blocking collectives: 27.3 us -> 0 us
  starting transfers between devices: 0.04 us -> 17.3 us
  between operations: 13.6 us -> 0.2 us
  matrix products: 11.8 us -> 1.54 us
  Pallas kernels: 0 us -> 9.62 us
  local copies, waits for them, and re-layouts: 15.1 us -> 7.21 us
  other arithmetic: 5.74 us -> 2.48 us
    reduce_scatter x1 -> x0, waiting for transfers between devices: 65.1 us -> none  [body(): lax.psum_scatter(jnp.dot(columns, kv_weight, preferred_element_type=jnp.f...]
    ppermute x0 -> x15, waiting for transfers between devices: none -> 36.8 us  [the longest x9 23.2 us: swap_plane(): return lax.ppermute(x, 'blk', [(i, i ^ step * LANE) for i in range(n_blk)])]
    all_gather x1 -> x0, waiting for transfers between devices: 34.7 us -> none  [body(): arrived = lax.all_gather(kv_rows_local, 'blk', axis=0, tiled=True)]
    all_to_all x1 -> x0, blocking collectives: 27.3 us -> none  [body(): lax.all_to_all(image_states, 'blk', split_axis=1, concat_axis=0, tiled=True)]
    ppermute x0 -> x15, starting transfers between devices: none -> 17.3 us  [the longest x9 13.4 us: swap_plane(): return lax.ppermute(x, 'blk', [(i, i ^ step * LANE) for i in range(n_blk)])]
    dot_general x5 -> x4, matrix products: 11.8 us -> 1.54 us  [body(): jnp.dot(columns, weights[j], preferred_element_type=jnp.float32)]
    pallas_call x0 -> x2, Pallas kernels: none -> 9.62 us  [the longest x1 6.78 us: attend(): pl.pallas_call(functools.partial(attend_kernel, group_size, head_dim, len...]
    reshape x5 -> x0, local copies, waits for them, and re-layouts: 7.18 us -> none  [the longest x2 3.13 us: body(): key_block[:, kv_width:].reshape(block_size, kv_heads, head_dim)]
  transfers between devices with their start and end apart: 2 -> 15, of which waited for: 2 -> 10; matrix products, arithmetic and copies ran while one was open for 2% -> 11% of each run, Pallas kernels for 0% -> 4%
where the time goes in v1:
time: 75.4 us; the launch traced here: 75.1 us
  waiting for transfers between devices  36.8 us (49%)
  starting transfers between devices  17.3 us (23%)
  Pallas kernels  9.62 us (13%)
  local copies, waits for them, and re-layouts  7.21 us (10%)
  other arithmetic  2.48 us (3%)
  matrix products  1.54 us (2%)
    ppermute x9, waiting for transfers between devices, swap_plane(): return lax.ppermute(x, 'blk', [(i, i ^ step * LANE) for i in range(n_blk)])  23.2 us
    ppermute x6, waiting for transfers between devices, swap_lane(): return lax.ppermute(x, 'blk', [(i, i ^ bits) for i in range(n_blk)])  13.6 us
    ppermute x9, starting transfers between devices, swap_plane(): return lax.ppermute(x, 'blk', [(i, i ^ step * LANE) for i in range(n_blk)])  13.4 us
    pallas_call x1, Pallas kernels, attend(): pl.pallas_call(functools.partial(attend_kernel, group_size, head_dim, len...  6.78 us
    unnamed x19, local copies, waits for them, and re-layouts  3.99 us
    ppermute x6, starting transfers between devices, swap_lane(): return lax.ppermute(x, 'blk', [(i, i ^ bits) for i in range(n_blk)])  3.89 us
    pallas_call x1, Pallas kernels, norm_queries(): pl.pallas_call(functools.partial(norm_kernel, width // head_dim, head_dim...  2.84 us
    dynamic_slice x1, local copies, waits for them, and re-layouts, body(): lax.dynamic_slice_in_dim(image_states, (plane ^ step) * span, span, 1)  2.03 us
  transfers between devices with their start and end apart: 15, of which 10 were waited for; matrix products, arithmetic and copies ran while one was open for 11% of the time, Pallas kernels for 4%

profile of v1, /device:TPU:0, one launch (start us, length us, event | category | flops | bytes accessed | tf_op | source)
XLA Modules:
  0.0 75.1 jit_solution(3942940398915993360)
XLA Ops:
  0.0 0.5 collective-permute-start.3
  0.5 2.5 %collective-permute-start.4 = (bf16[512,1024]{1,0:T(8,128)(2,1)}, bf16[512,1024]{1,0:T(8,128)(2,1)S(1)}, u32[]{:S(2)}, u32[]{:S(2)}) collective-permute-start(bf16[512,1024]{1,0:T(8,128)(2,1)} %param.9), channel_id=1, source_target_pairs={{0,2},{1,3},{2,0},{3,1},{4,6},{5,7},{6,4},{7,5},{8,10},{9,11},{10,... | collective-permute-start | bytes 3145736 | tf_op jit(solution)/shard_map/ppermute | solution.py:94
  3.0 2.0 %constant_dynamic-slice_fusion = (bf16[48,2048]{1,0:T(8,128)(2,1)S(1)}, bf16[48,2048]{1,0:T(8,128)(2,1)}, bf16[48,2048]{1,0:T(8,128)(2,1)S(1)}, bf16[48,2048]{1,0:T(8,128)(2,1)}) fusion(bf16[48,8192]{1,0:T(8,128)(2,1)} %param.8, s32[]{:T(128)S(6)} %select_n.43, s32[]{:T(128)S(6)} %select_n.41, s32[]{:T(128)S(6)} %select_n.40, s32[]{:T(128)S(6)} %select_n.42), kind=kLoop, calls=%fused_computation.35 | loop fusion | bytes 1572880 | tf_op jit(solution)/shard_map/dynamic_slice | solution.py:102
  5.0 1.6 %collective-permute-start = (bf16[48,2048]{1,0:T(8,128)(2,1)}, bf16[48,2048]{1,0:T(8,128)(2,1)}, u32[]{:S(2)}, u32[]{:S(2)}) collective-permute-start(bf16[48,2048]{1,0:T(8,128)(2,1)} %get-tuple-element.20), channel_id=1, source_target_pairs={{0,4},{1,5},{2,6},{3,7},{4,0},{5,1},{6,2},{7,3},{8,12},{9,13},{10,... | collective-permute-start | bytes 589832 | tf_op jit(solution)/shard_map/ppermute | solution.py:97
  6.6 2.6 %collective-permute-start.1 = (bf16[48,2048]{1,0:T(8,128)(2,1)}, bf16[48,2048]{1,0:T(8,128)(2,1)}, u32[]{:S(2)}, u32[]{:S(2)}) collective-permute-start(bf16[48,2048]{1,0:T(8,128)(2,1)} %get-tuple-element.22), channel_id=1, source_target_pairs={{0,8},{1,9},{2,10},{3,11},{4,12},{5,13},{6,14},{7,15},{8,0},{9,1},... | collective-permute-start | bytes 589832 | tf_op jit(solution)/shard_map/ppermute | solution.py:97
  9.2 0.2 collective-permute-start.2
  9.4 0.7 copy-done.5
  10.1 0.2 reduce-window.16
  10.3 0.1 add_multiply_fusion
  10.3 0.1 iota_add_fusion
  10.4 0.1 add.119
  10.5 0.7 copy-done.6
  11.2 0.2 reduce-window.17
  11.3 0.1 convert_reduce_fusion
  11.4 0.9 %select_convert_fusion.bias_ref = bf16[768,128]{1,0:T(8,128)(2,1)} fusion(s32[768]{0:T(1024)S(1)} %convert_reduce_fusion), kind=kLoop, calls=%fused_computation.4 | loop fusion | flops 294912 | bytes 199680 | tf_op jit(solution)/shard_map/convert_element_type | solution.py:119
  12.3 2.8 %norm_queries.1.q_ref = bf16[128,4096]{1,0:T(8,128)(2,1)} custom-call(bf16[128,4096]{1,0:T(8,128)(2,1)} %x_ref.1, f32[1,128]{1,0:T(1,128)} %bitcast.19), custom_call_target="tpu_custom_call" | custom-call | tf_op jit(solution)/shard_map/norm_queries/pallas_call | solution.py:27
  15.1 0.1 convert_reduce_fusion.1
  15.2 0.7 fusion.9.segment_ref
  15.9 0.1 collective-permute-done
  16.1 8.0 %collective-permute-done.1 = bf16[48,2048]{1,0:T(8,128)(2,1)} collective-permute-done((bf16[48,2048]{1,0:T(8,128)(2,1)}, bf16[48,2048]{1,0:T(8,128)(2,1)}, u32[]{:S(2)}, u32[]{:S(2)}) %collective-permute-start.1) | collective-permute-done | bytes 196640 | tf_op jit(solution)/shard_map/ppermute | solution.py:97
  24.0 0.9 %constant_dynamic-update-slice_fusion.2 = bf16[192,2048]{1,0:T(8,128)(2,1)S(1)} fusion(bf16[192,2048]{1,0:T(8,128)(2,1)S(1)} %constant_dynamic-update-slice_fusion.3, bf16[48,2048]{1,0:T(8,128)(2,1)} %collective-permute-done), kind=kLoop, calls=%fused_computation.26 | loop fusion | bytes 393216
  25.0 0.9 %constant_dynamic-update-slice_fusion.1 = bf16[192,2048]{1,0:T(8,128)(2,1)S(1)} fusion(bf16[192,2048]{1,0:T(8,128)(2,1)S(1)} %constant_dynamic-update-slice_fusion.2, bf16[48,2048]{1,0:T(8,128)(2,1)} %collective-permute-done.1), kind=kLoop, calls=%fused_computation.25 | loop fusion | bytes 393216
  25.9 1.1 %collective-permute-done.4 = bf16[512,1024]{1,0:T(8,128)(2,1)S(1)} collective-permute-done((bf16[512,1024]{1,0:T(8,128)(2,1)}, bf16[512,1024]{1,0:T(8,128)(2,1)S(1)}, u32[]{:S(2)}, u32[]{:S(2)}) %collective-permute-start.4) | collective-permute-done | bytes 1048608 | tf_op jit(solution)/shard_map/ppermute | solution.py:94
  27.0 0.9 %constant_dynamic-update-slice_fusion = bf16[192,2048]{1,0:T(8,128)(2,1)S(1)} fusion(bf16[192,2048]{1,0:T(8,128)(2,1)S(1)} %constant_dynamic-update-slice_fusion.1, bf16[48,2048]{1,0:T(8,128)(2,1)} %collective-permute-done.2), kind=kLoop, calls=%fused_computation.24 | loop fusion | bytes 393216 | tf_op jit(solution)/shard_map/concatenate | solution.py:124
  28.0 0.4 fusion.5
  28.4 0.0 collective-permute-done.3
  28.4 0.4 convolution_add_fusion.2
  28.8 0.4 convolution_add_fusion.1
  29.2 0.5 collective-permute-done.5
  29.7 0.4 fusion.15
  30.1 3.9 %collective-permute-start.8 = (bf16[48,1024]{1,0:T(8,128)(2,1)S(1)}, bf16[48,1024]{1,0:T(8,128)(2,1)S(1)}, u32[]{:S(2)}, u32[]{:S(2)}) collective-permute-start(bf16[48,1024]{1,0:T(8,128)(2,1)S(1)} %get-tuple-element.24), channel_id=1, source_target_pairs={{0,12},{1,13},{2,14},{3,15},{4,8},{5,9},{6,10},{7,11},{8,4},{9,5},... | collective-permute-start | bytes 294920 | tf_op jit(solution)/shard_map/ppermute | solution.py:97
  34.0 0.4 collective-permute-start.7
  34.4 0.2 collective-permute-start.6
  34.7 2.6 %collective-permute-done.8 = bf16[48,1024]{1,0:T(8,128)(2,1)S(1)} collective-permute-done((bf16[48,1024]{1,0:T(8,128)(2,1)S(1)}, bf16[48,1024]{1,0:T(8,128)(2,1)S(1)}, u32[]{:S(2)}, u32[]{:S(2)}) %collective-permute-start.8) | collective-permute-done | bytes 98336 | tf_op jit(solution)/shard_map/ppermute | solution.py:97
  37.3 6.2 %collective-permute-done.7 = bf16[48,1024]{1,0:T(8,128)(2,1)S(1)} collective-permute-done((bf16[48,1024]{1,0:T(8,128)(2,1)S(1)}, bf16[48,1024]{1,0:T(8,128)(2,1)S(1)}, u32[]{:S(2)}, u32[]{:S(2)}) %collective-permute-start.7) | collective-permute-done | bytes 98336 | tf_op jit(solution)/shard_map/ppermute | solution.py:97
  43.4 0.0 collective-permute-done.6
  43.4 0.1 fusion.1
  43.6 0.1 reduce_sum.29
  43.7 0.1 mul.92
  43.9 2.7 %collective-permute-start.11 = (bf16[48,1024]{1,0:T(8,128)(2,1)S(1)}, bf16[48,1024]{1,0:T(8,128)(2,1)S(1)}, u32[]{:S(2)}, u32[]{:S(2)}) collective-permute-start(bf16[48,1024]{1,0:T(8,128)(2,1)S(1)} %pad_maximum_fusion.1), channel_id=1, source_target_pairs={{0,12},{1,13},{2,14},{3,15},{4,8},{5,9},{6,10},{7,11},{8,4},{9,5},... | collective-permute-start | bytes 294920 | tf_op jit(solution)/shard_map/ppermute | solution.py:97
  46.5 1.8 %collective-permute-start.9 = (bf16[48,1024]{1,0:T(8,128)(2,1)S(1)}, bf16[48,1024]{1,0:T(8,128)(2,1)S(1)}, u32[]{:S(2)}, u32[]{:S(2)}) collective-permute-start(bf16[48,1024]{1,0:T(8,128)(2,1)S(1)} %pad_maximum_fusion.1), channel_id=1, source_target_pairs={{0,4},{1,5},{2,6},{3,7},{4,0},{5,1},{6,2},{7,3},{8,12},{9,13},{10,... | collective-permute-start | bytes 294920 | tf_op jit(solution)/shard_map/ppermute | solution.py:97
  48.3 3.2 %collective-permute-done.11 = bf16[48,1024]{1,0:T(8,128)(2,1)S(1)} collective-permute-done((bf16[48,1024]{1,0:T(8,128)(2,1)S(1)}, bf16[48,1024]{1,0:T(8,128)(2,1)S(1)}, u32[]{:S(2)}, u32[]{:S(2)}) %collective-permute-start.11) | collective-permute-done | bytes 98336 | tf_op jit(solution)/shard_map/ppermute | solution.py:97
  51.5 3.2 %collective-permute-done.10 = bf16[48,1024]{1,0:T(8,128)(2,1)S(1)} collective-permute-done((bf16[48,1024]{1,0:T(8,128)(2,1)S(1)}, bf16[48,1024]{1,0:T(8,128)(2,1)S(1)}, u32[]{:S(2)}, u32[]{:S(2)}) %collective-permute-start.10) | collective-permute-done | bytes 98336 | tf_op jit(solution)/shard_map/ppermute | solution.py:97
  54.7 0.9 %collective-permute-start.13 = (bf16[192,1024]{1,0:T(8,128)(2,1)S(1)}, bf16[192,1024]{1,0:T(8,128)(2,1)S(1)}, u32[]{:S(2)}, u32[]{:S(2)}) collective-permute-start(bf16[192,1024]{1,0:T(8,128)(2,1)S(1)} %pad_maximum_fusion.refs_0_.refs_4_), channel_id=1, source_target_pairs={{0,2},{1,3},{2,0},{3,1},{4,6},{5,7},{6,4},{7,5},{8,10},{9,11},{10,... | collective-permute-start | bytes 1179656 | tf_op jit(solution)/shard_map/ppermute | solution.py:94
  55.6 10.2 %collective-permute-done.13.refs_2_.refs_6_ = bf16[192,1024]{1,0:T(8,128)(2,1)S(1)} collective-permute-done((bf16[192,1024]{1,0:T(8,128)(2,1)S(1)}, bf16[192,1024]{1,0:T(8,128)(2,1)S(1)}, u32[]{:S(2)}, u32[]{:S(2)}) %collective-permute-start.13) | collective-permute-done | bytes 393248 | tf_op jit(solution)/shard_map/ppermute | solution.py:94
  65.8 1.7 %collective-permute-done.14.refs_3_.refs_7_ = bf16[192,1024]{1,0:T(8,128)(2,1)S(1)} collective-permute-done((bf16[192,1024]{1,0:T(8,128)(2,1)S(1)}, bf16[192,1024]{1,0:T(8,128)(2,1)S(1)}, u32[]{:S(2)}, u32[]{:S(2)}) %collective-permute-start.14) | collective-permute-done | bytes 393248 | tf_op jit(solution)/shard_map/ppermute | solution.py:94
  67.6 0.7 copy-done.3
  68.3 6.8 %attend.1 = bf16[128,4096]{1,0:T(8,128)(2,1)} custom-call(bf16[128,4096]{1,0:T(8,128)(2,1)} %norm_queries.1.q_ref, bf16[128,128]{1,0:T(8,128)(2,1)} %fusion.9.segment_ref, bf16[768,128]{1,0:T(8,128)(2,1)} %select_convert_fusion.bias_ref, bf16[192,1024]{1,0:T(8,128)(2,1)} %copy-done, bf16[192,1024]{1,0:T(8,128)(2,1)} %copy-done.2, ...), custom_call_target="tpu_custom_call" | custom-call | tf_op jit(solution)/shard_map/attend/pallas_call | solution.py:65
  (33 shorter events, 0.2 us)
Async XLA Ops:
  0.0 28.4 %collective-permute-start.3 = (bf16[512,1024]{1,0:T(8,128)(2,1)}, bf16[512,1024]{1,0:T(8,128)(2,1)S(1)}, u32[]{:S(2)}, u32[]{:S(2)}) collective-permute-start(bf16[512,1024]{1,0:T(8,128)(2,1)} %param.9), channel_id=1, source_target_pairs={{0,1},{1,0},{2,3},{3,2},{4,5},{5,4},{6,7},{7,6},{8,9},{9,8},{10,11... | collective-permute-start | bytes 3145736 | tf_op jit(solution)/shard_map/ppermute | solution.py:94
  0.5 26.5 %collective-permute-start.4 = (bf16[512,1024]{1,0:T(8,128)(2,1)}, bf16[512,1024]{1,0:T(8,128)(2,1)S(1)}, u32[]{:S(2)}, u32[]{:S(2)}) collective-permute-start(bf16[512,1024]{1,0:T(8,128)(2,1)} %param.9), channel_id=1, source_target_pairs={{0,2},{1,3},{2,0},{3,1},{4,6},{5,7},{6,4},{7,5},{8,10},{9,11},{10,... | collective-permute-start | bytes 3145736 | tf_op jit(solution)/shard_map/ppermute | solution.py:94
  5.0 11.0 %collective-permute-start = (bf16[48,2048]{1,0:T(8,128)(2,1)}, bf16[48,2048]{1,0:T(8,128)(2,1)}, u32[]{:S(2)}, u32[]{:S(2)}) collective-permute-start(bf16[48,2048]{1,0:T(8,128)(2,1)} %get-tuple-element.20), channel_id=1, source_target_pairs={{0,4},{1,5},{2,6},{3,7},{4,0},{5,1},{6,2},{7,3},{8,12},{9,13},{10,... | collective-permute-start | bytes 589832 | tf_op jit(solution)/shard_map/ppermute | solution.py:97
  6.6 17.4 %collective-permute-start.1 = (bf16[48,2048]{1,0:T(8,128)(2,1)}, bf16[48,2048]{1,0:T(8,128)(2,1)}, u32[]{:S(2)}, u32[]{:S(2)}) collective-permute-start(bf16[48,2048]{1,0:T(8,128)(2,1)} %get-tuple-element.22), channel_id=1, source_target_pairs={{0,8},{1,9},{2,10},{3,11},{4,12},{5,13},{6,14},{7,15},{8,0},{9,1},... | collective-permute-start | bytes 589832 | tf_op jit(solution)/shard_map/ppermute | solution.py:97
  9.2 14.8 %collective-permute-start.2 = (bf16[48,2048]{1,0:T(8,128)(2,1)S(1)}, bf16[48,2048]{1,0:T(8,128)(2,1)}, u32[]{:S(2)}, u32[]{:S(2)}) collective-permute-start(bf16[48,2048]{1,0:T(8,128)(2,1)S(1)} %get-tuple-element.19), channel_id=1, source_target_pairs={{0,12},{1,13},{2,14},{3,15},{4,8},{5,9},{6,10},{7,11},{8,4},{9,5},... | collective-permute-start | bytes 589832 | tf_op jit(solution)/shard_map/ppermute | solution.py:97
  9.4 0.7 copy-start.5
  10.5 0.7 copy-start.6
  12.3 3.6 %copy-start.7 = (f32[128]{0:T(128)S(1)}, f32[128]{0:T(128)}, u32[]{:S(2)}) copy-start(f32[128]{0:T(128)} %param.11) | copy-start | bytes 1540
  15.1 12.9 %copy-start.4 = (bf16[512,1024]{1,0:T(8,128)(2,1)S(1)}, bf16[512,1024]{1,0:T(8,128)(2,1)}, u32[]{:S(2)}) copy-start(bf16[512,1024]{1,0:T(8,128)(2,1)} %param.9) | copy-start | bytes 3145732
  27.0 2.7 %collective-permute-start.5 = (bf16[512,1024]{1,0:T(8,128)(2,1)S(1)}, bf16[512,1024]{1,0:T(8,128)(2,1)S(1)}, u32[]{:S(2)}, u32[]{:S(2)}) collective-permute-start(bf16[512,1024]{1,0:T(8,128)(2,1)S(1)} %collective-permute-done.4), channel_id=1, source_target_pairs={{0,1},{1,0},{2,3},{3,2},{4,5},{5,4},{6,7},{7,6},{8,9},{9,8},{10,11... | collective-permute-start | bytes 3145736 | tf_op jit(solution)/shard_map/ppermute | solution.py:94
  30.1 7.1 %collective-permute-start.8 = (bf16[48,1024]{1,0:T(8,128)(2,1)S(1)}, bf16[48,1024]{1,0:T(8,128)(2,1)S(1)}, u32[]{:S(2)}, u32[]{:S(2)}) collective-permute-start(bf16[48,1024]{1,0:T(8,128)(2,1)S(1)} %get-tuple-element.24), channel_id=1, source_target_pairs={{0,12},{1,13},{2,14},{3,15},{4,8},{5,9},{6,10},{7,11},{8,4},{9,5},... | collective-permute-start | bytes 294920 | tf_op jit(solution)/shard_map/ppermute | solution.py:97
  34.0 9.4 %collective-permute-start.7 = (bf16[48,1024]{1,0:T(8,128)(2,1)S(1)}, bf16[48,1024]{1,0:T(8,128)(2,1)S(1)}, u32[]{:S(2)}, u32[]{:S(2)}) collective-permute-start(bf16[48,1024]{1,0:T(8,128)(2,1)S(1)} %get-tuple-element.25), channel_id=1, source_target_pairs={{0,8},{1,9},{2,10},{3,11},{4,12},{5,13},{6,14},{7,15},{8,0},{9,1},... | collective-permute-start | bytes 294920 | tf_op jit(solution)/shard_map/ppermute | solution.py:97
  34.4 9.0 %collective-permute-start.6 = (bf16[48,1024]{1,0:T(8,128)(2,1)S(1)}, bf16[48,1024]{1,0:T(8,128)(2,1)S(1)}, u32[]{:S(2)}, u32[]{:S(2)}) collective-permute-start(bf16[48,1024]{1,0:T(8,128)(2,1)S(1)} %get-tuple-element.23), channel_id=1, source_target_pairs={{0,4},{1,5},{2,6},{3,7},{4,0},{5,1},{6,2},{7,3},{8,12},{9,13},{10,... | collective-permute-start | bytes 294920 | tf_op jit(solution)/shard_map/ppermute | solution.py:97
  43.9 7.6 %collective-permute-start.11 = (bf16[48,1024]{1,0:T(8,128)(2,1)S(1)}, bf16[48,1024]{1,0:T(8,128)(2,1)S(1)}, u32[]{:S(2)}, u32[]{:S(2)}) collective-permute-start(bf16[48,1024]{1,0:T(8,128)(2,1)S(1)} %pad_maximum_fusion.1), channel_id=1, source_target_pairs={{0,12},{1,13},{2,14},{3,15},{4,8},{5,9},{6,10},{7,11},{8,4},{9,5},... | collective-permute-start | bytes 294920 | tf_op jit(solution)/shard_map/ppermute | solution.py:97
  46.5 8.2 %collective-permute-start.10 = (bf16[48,1024]{1,0:T(8,128)(2,1)S(1)}, bf16[48,1024]{1,0:T(8,128)(2,1)S(1)}, u32[]{:S(2)}, u32[]{:S(2)}) collective-permute-start(bf16[48,1024]{1,0:T(8,128)(2,1)S(1)} %pad_maximum_fusion.1), channel_id=1, source_target_pairs={{0,8},{1,9},{2,10},{3,11},{4,12},{5,13},{6,14},{7,15},{8,0},{9,1},... | collective-permute-start | bytes 294920 | tf_op jit(solution)/shard_map/ppermute | solution.py:97
  46.5 8.2 %collective-permute-start.9 = (bf16[48,1024]{1,0:T(8,128)(2,1)S(1)}, bf16[48,1024]{1,0:T(8,128)(2,1)S(1)}, u32[]{:S(2)}, u32[]{:S(2)}) collective-permute-start(bf16[48,1024]{1,0:T(8,128)(2,1)S(1)} %pad_maximum_fusion.1), channel_id=1, source_target_pairs={{0,4},{1,5},{2,6},{3,7},{4,0},{5,1},{6,2},{7,3},{8,12},{9,13},{10,... | collective-permute-start | bytes 294920 | tf_op jit(solution)/shard_map/ppermute | solution.py:97
  54.7 12.8 %copy-start = (bf16[192,1024]{1,0:T(8,128)(2,1)}, bf16[192,1024]{1,0:T(8,128)(2,1)S(1)}, u32[]{:S(2)}) copy-start(bf16[192,1024]{1,0:T(8,128)(2,1)S(1)} %pad_maximum_fusion.refs_0_.refs_4_) | copy-start | bytes 1179652
  54.7 11.1 %collective-permute-start.13 = (bf16[192,1024]{1,0:T(8,128)(2,1)S(1)}, bf16[192,1024]{1,0:T(8,128)(2,1)S(1)}, u32[]{:S(2)}, u32[]{:S(2)}) collective-permute-start(bf16[192,1024]{1,0:T(8,128)(2,1)S(1)} %pad_maximum_fusion.refs_0_.refs_4_), channel_id=1, source_target_pairs={{0,2},{1,3},{2,0},{3,1},{4,6},{5,7},{6,4},{7,5},{8,10},{9,11},{10,... | collective-permute-start | bytes 1179656 | tf_op jit(solution)/shard_map/ppermute | solution.py:94
  55.6 10.2 %collective-permute-start.12 = (bf16[192,1024]{1,0:T(8,128)(2,1)S(1)}, bf16[192,1024]{1,0:T(8,128)(2,1)S(1)}, u32[]{:S(2)}, u32[]{:S(2)}) collective-permute-start(bf16[192,1024]{1,0:T(8,128)(2,1)S(1)} %pad_maximum_fusion.refs_0_.refs_4_), channel_id=1, source_target_pairs={{0,1},{1,0},{2,3},{3,2},{4,5},{5,4},{6,7},{7,6},{8,9},{9,8},{10,11... | collective-permute-start | bytes 1179656 | tf_op jit(solution)/shard_map/ppermute | solution.py:94
  65.8 1.7 %copy-start.1 = (bf16[192,1024]{1,0:T(8,128)(2,1)}, bf16[192,1024]{1,0:T(8,128)(2,1)S(1)}, u32[]{:S(2)}) copy-start(bf16[192,1024]{1,0:T(8,128)(2,1)S(1)} %collective-permute-done.13.refs_2_.refs_6_) | copy-start | bytes 1179652
  65.8 1.7 %collective-permute-start.14 = (bf16[192,1024]{1,0:T(8,128)(2,1)S(1)}, bf16[192,1024]{1,0:T(8,128)(2,1)S(1)}, u32[]{:S(2)}, u32[]{:S(2)}) collective-permute-start(bf16[192,1024]{1,0:T(8,128)(2,1)S(1)} %collective-permute-done.13.refs_2_.refs_6_), channel_id=1, source_target_pairs={{0,1},{1,0},{2,3},{3,2},{4,5},{5,4},{6,7},{7,6},{8,9},{9,8},{10,11... | collective-permute-start | bytes 1179656 | tf_op jit(solution)/shard_map/ppermute | solution.py:94
  65.8 1.7 %copy-start.2 = (bf16[192,1024]{1,0:T(8,128)(2,1)}, bf16[192,1024]{1,0:T(8,128)(2,1)S(1)}, u32[]{:S(2)}) copy-start(bf16[192,1024]{1,0:T(8,128)(2,1)S(1)} %collective-permute-done.12.refs_1_.refs_5_) | copy-start | bytes 1179652
  67.6 0.8 %copy-start.3 = (bf16[192,1024]{1,0:T(8,128)(2,1)}, bf16[192,1024]{1,0:T(8,128)(2,1)S(1)}, u32[]{:S(2)}) copy-start(bf16[192,1024]{1,0:T(8,128)(2,1)S(1)} %collective-permute-done.14.refs_3_.refs_7_) | copy-start | bytes 1179652
